TPU v7x, 32 devices: a whole 2x2x4 slice. The times are simulated.
32 devices in a mesh: parts: 2 (over x), seq: 16 (over z, y, core).
Axes of the slice: x: 2, y: 2, z: 4, core: 2. Of those that a mesh axis runs over, the one named last changes fastest.
Arguments:
- prefix_latent: bfloat16 [61440, 512], P(('parts', 'seq')), parts along dimension 0, may hold values from -6 to 6
- block_order: int32 [480], P(('parts', 'seq')), parts along dimension 0, may hold values from 0 to 239, each once
- key_up: bfloat16 [512, 512], replicated, may hold values from -0.25 to 0.25
- value_up: bfloat16 [512, 512], replicated, may hold values from -0.25 to 0.25
- queries: bfloat16 [32, 4, 4096], P(('parts', 'seq')), parts along dimension 0, may hold values from -200 to 200
- new_keys: bfloat16 [32, 4, 512], P(('parts', 'seq')), parts along dimension 0, may hold values from -6 to 6
- new_values: bfloat16 [32, 4, 512], P(('parts', 'seq')), parts along dimension 0, may hold values from -6 to 6
- suffix_keys: bfloat16 [32, 4096, 512], P(('parts', 'seq')), parts along dimension 0, may hold values from -6 to 6
- suffix_values: bfloat16 [32, 4096, 512], P(('parts', 'seq')), parts along dimension 0, may hold values from -6 to 6
- suffix_len: int32 [32], P(('parts', 'seq')), parts along dimension 0, may hold values from 1 to 4096, 32768 in all
Outputs:
- attended: bfloat16 [32, 4, 4096], P(('parts', 'seq')), parts along dimension 0
There are 2 independent parts, one for each index of `parts`. A program takes and returns all parts, laid end to end along the dimension named above; an argument that names none is the same for every part. Nothing has to cross between parts.
Inputs may be any that keep to these rules, and one draw needn't show every extreme that they name: A request's cache holds its first suffix_len entries; some request holds exactly 4096. `block_order`: each block position appears once.
All inputs are finite; a program needn't handle non-finite values. No bound on the sum of `suffix_len` on one device may be relied on, other than what follows from the above.
Results may differ from a plain program's by a relative error of at most 0.005.
The roundings to bfloat16 on the way count: a program that leaves them out, or rounds other values in their place, can miss the bound.
Values may be sent and summed in bfloat16 or wider, within the bound.
No kernel may reach another device: no remote copies, remote signals or barrier semaphores. Data moves between devices by JAX's collectives and lax.ppermute only.
A program may use at most 128 MiB of HBM per device.

v0:
```python
import math
import jax
import jax.numpy as jnp
import numpy as np
from jax import lax
from jax.sharding import PartitionSpec as P

HD = 128
QH = 32
KVH = 4
BLK = 128
STEPS = 4
SUF = 4096


def phase_table(half):
    index = np.arange(half)
    freq = 500000.0 ** (-2.0 * index / (2 * half))
    mult = np.floor(2.0**24 * freq / (2 * np.pi)).astype(np.int64)
    return ((mult >> 12).astype(np.int32), (mult & 4095).astype(np.int32))


def rotate(values, position):
    half = values.shape[-1] // 2
    high, low = phase_table(half)
    spot = position[..., None]
    first = spot * jnp.asarray(low, dtype=jnp.int32)
    second = spot * jnp.asarray(high, dtype=jnp.int32) % 4096
    turns = (first + second * 4096) % 16777216
    angle = turns.astype(values.dtype) * (2.0 * math.pi / 16777216.0)
    cosine = jnp.cos(angle)[..., None, :]
    sine = jnp.sin(angle)[..., None, :]
    lower = values[..., :half]
    upper = values[..., half:]
    return jnp.concatenate([lower * cosine - upper * sine, upper * cosine + lower * sine], -1)


def local(
    prefix_latent,
    block_order,
    key_up,
    value_up,
    queries,
    new_keys,
    new_values,
    suffix_keys,
    suffix_values,
    suffix_len,
):
    seq_count = lax.axis_size("seq")
    pre_rows = prefix_latent.shape[0]
    prefix = pre_rows * seq_count
    req_rows = queries.shape[0]
    group = QH // KVH
    scale = 1.0 / math.sqrt(HD)
    rows = jnp.arange(pre_rows, dtype=jnp.int32)
    key_pos = jnp.repeat(block_order, BLK) * BLK + rows % BLK
    keys = jnp.dot(prefix_latent, key_up, preferred_element_type=jnp.float32).reshape(
        pre_rows, KVH, HD
    )
    keys = rotate(keys, key_pos).astype(jnp.bfloat16)
    values = (
        jnp.dot(prefix_latent, value_up, preferred_element_type=jnp.float32)
        .astype(jnp.bfloat16)
        .reshape(pre_rows, KVH, HD)
    )
    step_index = jnp.arange(STEPS, dtype=jnp.int32)
    query_pos = prefix + suffix_len[:, None] + step_index[None, :]
    query_rot = rotate(
        queries.astype(jnp.float32).reshape(req_rows, STEPS, QH, HD), query_pos
    ).astype(jnp.bfloat16)
    new_rot = rotate(
        new_keys.astype(jnp.float32).reshape(req_rows, STEPS, KVH, HD), query_pos
    ).astype(jnp.bfloat16)

    def shard_part(query_block):
        count = query_block.shape[0]
        width = query_block.shape[1]
        split = query_block.reshape(count, width, KVH, group, HD)
        scores = (
            jnp.einsum("rtkgd,pkd->rtkgp", split, keys, preferred_element_type=jnp.float32) * scale
        )
        peak = jnp.max(scores, -1)
        expo = jnp.exp(scores - peak[..., None])
        total = jnp.sum(expo, -1)
        summed = jnp.einsum(
            "rtkgp,pkd->rtkgd",
            expo.astype(jnp.bfloat16),
            values,
            preferred_element_type=jnp.float32,
        )
        part = summed / total[..., None]
        return (
            part.reshape(count, width, QH * HD),
            peak.reshape(count, width, QH),
            total.reshape(count, width, QH),
        )

    def prefix_attention(selected):
        width = selected.shape[1]
        whole = lax.all_gather(selected, "seq", axis=0, tiled=True)
        count = whole.shape[0]
        per_block = math.gcd(count, max(1, 512 // (width * QH)))
        blocks = whole.reshape(count // per_block, per_block, width, QH * HD)
        parts, peaks, totals = lax.map(shard_part, blocks)
        parts = parts.reshape(count, width, QH * HD)
        peaks = peaks.reshape(count, width, QH)
        totals = totals.reshape(count, width, QH)
        got_parts, got_peaks, got_totals = (
            lax.all_to_all(parts[:, None], "seq", split_axis=0, concat_axis=1, tiled=True),
            lax.all_to_all(peaks[:, None], "seq", split_axis=0, concat_axis=1, tiled=True),
            lax.all_to_all(totals[:, None], "seq", split_axis=0, concat_axis=1, tiled=True),
        )
        highest = jnp.max(got_peaks, 1)
        factor = got_totals * jnp.exp(got_peaks - highest[:, None])
        numer = jnp.sum(
            factor[..., None] * got_parts.reshape(req_rows, seq_count, width, QH, HD), 1
        )
        denom = jnp.sum(factor, 1)
        return (highest, numer, denom)

    flat_queries = query_rot.reshape(req_rows, STEPS, QH * HD)
    results = [prefix_attention(flat_queries[:, which : which + 1]) for which in range(STEPS)]
    highest = jnp.concatenate([entry[0] for entry in results], 1)
    numer = jnp.concatenate([entry[1] for entry in results], 1)
    denom = jnp.concatenate([entry[2] for entry in results], 1)
    split = query_rot.reshape(req_rows, STEPS, KVH, group, HD)
    cache_keys = suffix_keys.reshape(req_rows, SUF, KVH, HD)
    cache_values = suffix_values.reshape(req_rows, SUF, KVH, HD)
    cache_scores = (
        jnp.einsum("rtkgd,rpkd->rtkgp", split, cache_keys, preferred_element_type=jnp.float32)
        * scale
    )
    live = jnp.arange(SUF, dtype=jnp.int32)[None, :] < suffix_len[:, None]
    cache_scores = jnp.where(live[:, None, None, None, :], cache_scores, -jnp.inf)
    fresh_keys = new_rot.reshape(req_rows, STEPS, KVH, HD)
    fresh_values = new_values.reshape(req_rows, STEPS, KVH, HD)
    fresh_scores = (
        jnp.einsum("rtkgd,rukd->rtkgu", split, fresh_keys, preferred_element_type=jnp.float32)
        * scale
    )
    causal = step_index[:, None] >= step_index[None, :]
    fresh_scores = jnp.where(causal[None, :, None, None, :], fresh_scores, -jnp.inf)
    local_peak = jnp.maximum(jnp.max(cache_scores, -1), jnp.max(fresh_scores, -1))
    cache_exp = jnp.exp(cache_scores - local_peak[..., None])
    fresh_exp = jnp.exp(fresh_scores - local_peak[..., None])
    local_total = jnp.sum(cache_exp, -1) + jnp.sum(fresh_exp, -1)
    local_numer = jnp.einsum(
        "rtkgp,rpkd->rtkgd",
        cache_exp.astype(jnp.bfloat16),
        cache_values,
        preferred_element_type=jnp.float32,
    )
    local_numer = local_numer + jnp.einsum(
        "rtkgu,rukd->rtkgd",
        fresh_exp.astype(jnp.bfloat16),
        fresh_values,
        preferred_element_type=jnp.float32,
    )
    local_peak = local_peak.reshape(req_rows, STEPS, QH)
    local_total = local_total.reshape(req_rows, STEPS, QH)
    local_numer = local_numer.reshape(req_rows, STEPS, QH, HD)
    biggest = jnp.maximum(highest, local_peak)
    prefix_weight = jnp.exp(highest - biggest)
    local_weight = jnp.exp(local_peak - biggest)
    result = (numer * prefix_weight[..., None] + local_numer * local_weight[..., None]) / (
        denom * prefix_weight + local_total * local_weight
    )[..., None]
    return result.reshape(req_rows, STEPS, QH * HD).astype(jnp.bfloat16)


def solution(mesh):
    placed = (
        P(("parts", "seq"), None),
        P(("parts", "seq")),
        P(),
        P(),
        P(("parts", "seq"), None, None),
        P(("parts", "seq"), None, None),
        P(("parts", "seq"), None, None),
        P(("parts", "seq"), None, None),
        P(("parts", "seq"), None, None),
        P(("parts", "seq")),
    )
    return jax.shard_map(
        local,
        mesh=mesh,
        in_specs=placed,
        out_specs=P(("parts", "seq"), None, None),
        check_vma=False,
    )
```

profile of v0, /device:TPU:0, one launch (start us, length us, event | category | flops | bytes accessed | tf_op | source)
XLA Modules:
  0.0 271.2 jit_solution(17228398530204130083)
XLA Ops:
  0.8 0.8 convert_bitcast_fusion
  1.6 0.8 fusion.115
  3.2 23.8 %all_gather.12 = bf16[16,1,4096]{2,1,0:T(2,128)(2,1)S(1)} all-gather(bf16[1,1,4096]{2,1,0:T(2,128)(2,1)S(1)} %get-tuple-element.75), channel_id=1, replica_groups=mesh['parts'=2,'seq'=16] {'seq'}, dimensions={0}, use_global_device_ids=true | all-gather | bytes 139264 | tf_op jit(solution)/shard_map/all_gather | solution.py:101
  27.0 0.7 reduce.40
  27.7 2.4 fusion.127
  30.1 2.3 fusion.123
  32.5 3.7 %copy.155 = f32[1920,4,64]{2,0,1:T(8,128)} copy(f32[1920,4,64]{0,2,1:T(8,128)} %get-tuple-element.72) | data formatting | bytes 3932160
  36.1 3.7 %copy.156 = f32[1920,4,64]{2,0,1:T(8,128)} copy(f32[1920,4,64]{0,2,1:T(8,128)} %get-tuple-element.71) | data formatting | bytes 3932160
  39.9 4.3 %fusion.77 = (f32[1920,64]{1,0:T(8,128)S(1)}, f32[1920,64]{1,0:T(8,128)S(1)}) fusion(s32[64]{0:T(128)S(1)} %copy-done.20, s32[64]{0:T(128)S(1)} %copy-done.19, s32[1920]{0:T(1024)S(1)} %fusion.96), kind=kLoop, calls=%fused_computation.80 | loop fusion | flops 3440640 | bytes 991232 | tf_op jit(solution)/shard_map/cos | solution.py:31
  44.3 4.5 %subtract_convert_fusion = (bf16[1920,4,64]{2,0,1:T(8,128)(2,1)S(1)}, bf16[1920,4,64]{2,0,1:T(8,128)(2,1)S(1)}) fusion(f32[1920,4,64]{2,0,1:T(8,128)} %copy.156, f32[1920,4,64]{2,0,1:T(8,128)} %copy.155, f32[1920,64]{1,0:T(8,128)S(1)} %get-tuple-element.89, f32[1920,64]{1,0:T(8,128)S(1)} %get-tuple-element.88), kind=kLoop, calls=%fused_computation.20 | loop fusion | flops 3932160 | bytes 6881280 | tf_op jit(solution)/shard_map/convert.12
  48.7 1.1 maximum_bitcast_fusion
  49.8 0.8 bitcast_reduce_fusion.3
  51.1 1.9 copy-done.4
  53.0 0.8 fusion.11
  54.4 3.7 %all-to-all-start = ((f32[16,1,1,32]{3,2,1,0:T(1,128)}), f32[16,1,1,32]{3,2,1,0:T(1,128)S(1)}, u32[]{:S(2)}, u32[]{:S(2)}) async-start(f32[16,1,1,32]{3,2,1,0:T(1,128)} %copy.101), calls=%async_computation | async-start | bytes 16384 | tf_op jit(solution)/shard_map/all_to_all | solution.py:112
  58.1 1.3 convolution_convert_fusion
  59.4 0.8 copy-done.5
  60.2 0.8 fusion.64
  61.1 22.2 %all_gather.13 = bf16[16,1,4096]{2,1,0:T(2,128)(2,1)S(1)} all-gather(bf16[1,1,4096]{2,1,0:T(2,128)(2,1)S(1)} %get-tuple-element.85), channel_id=1, replica_groups=mesh['parts'=2,'seq'=16] {'seq'}, dimensions={0}, use_global_device_ids=true | all-gather | bytes 139264 | tf_op jit(solution)/shard_map/all_gather | solution.py:101
  83.3 0.7 reduce.41
  84.0 0.8 bitcast_reduce_fusion.2
  84.9 0.8 fusion.13
  85.6 0.8 copy-done.24
  86.4 0.8 fusion.61
  87.2 18.2 %all_gather.14 = bf16[16,1,4096]{2,1,0:T(2,128)(2,1)S(1)} all-gather(bf16[1,1,4096]{2,1,0:T(2,128)(2,1)S(1)} %get-tuple-element.84), channel_id=1, replica_groups=mesh['parts'=2,'seq'=16] {'seq'}, dimensions={0}, use_global_device_ids=true | all-gather | bytes 139264 | tf_op jit(solution)/shard_map/all_gather | solution.py:101
  105.4 0.7 reduce.42
  106.2 0.8 bitcast_reduce_fusion.1
  107.0 0.8 fusion.15
  107.8 0.8 copy-done.25
  108.5 0.8 fusion.58
  109.4 19.5 %all_gather.15 = bf16[16,1,4096]{2,1,0:T(2,128)(2,1)S(1)} all-gather(bf16[1,1,4096]{2,1,0:T(2,128)(2,1)S(1)} %get-tuple-element.76), channel_id=1, replica_groups=mesh['parts'=2,'seq'=16] {'seq'}, dimensions={0}, use_global_device_ids=true | all-gather | bytes 139264 | tf_op jit(solution)/shard_map/all_gather | solution.py:101
  129.6 0.8 bitcast_reduce_fusion
  130.4 0.8 fusion.17
  131.2 0.8 copy-done.26
  132.0 0.8 fusion.55
  133.5 6.9 %reshape.1695 = bf16[4096,4,128]{2,1,0:T(4,128)(2,1)} reshape(bf16[1,4096,512]{2,1,0:T(8,128)(2,1)} %param.23) | data formatting | bytes 8388608 | tf_op jit(solution)/shard_map/reshape.165
  140.4 3.8 %all-to-all-start.1 = ((f32[16,1,1,32]{3,2,1,0:T(1,128)}), f32[16,1,1,32]{3,2,1,0:T(1,128)S(1)}, u32[]{:S(2)}, u32[]{:S(2)}) async-start(f32[16,1,1,32]{3,2,1,0:T(1,128)} %copy.102), calls=%async_computation.1 | async-start | bytes 16384 | tf_op jit(solution)/shard_map/all_to_all | solution.py:111
  144.2 3.8 %fusion.125 = (f32[4,4,8]{2,0,1:T(4,128)S(1)}, f32[1,4,4,8,4096]{4,3,1,2,0:T(8,128)S(1)}) fusion(bf16[4096,4,128,1]{2,1,0,3:T(4,128)(2,1)} %bitcast.286, pred[4096]{0:T(1024)(128)(4,1)S(1)} %iota_compare_fusion, bf16[4,4,8,64]{3,2,1,0:T(8,128)(2,1)S(1)} %bitcast.301, bf16[4,4,8,64]{3,2,1,0:T(8,128)(2,1)S(1)} %bitcast.299), kind=kOutput, calls=%fused_computation.167 | convolution fusion | flops 135856000 | bytes 6328832 | tf_op jit(solution)/shard_map/rtkgd,rpkd->rtkgp/dot_general | solution.py:131
  148.7 1.9 all-to-all-done.1
  150.6 4.1 %all-to-all-start.3 = ((f32[16,1,1,32]{3,2,1,0:T(1,128)}), f32[16,1,1,32]{3,2,1,0:T(1,128)S(1)}, u32[]{:S(2)}, u32[]{:S(2)}) async-start(f32[16,1,1,32]{3,2,1,0:T(1,128)} %copy.107), calls=%async_computation.3 | async-start | bytes 16384 | tf_op jit(solution)/shard_map/all_to_all | solution.py:112
  155.4 5.6 %all-to-all-done.3 = f32[16,1,1,32]{3,2,1,0:T(1,128)S(1)} async-done(((f32[16,1,1,32]{3,2,1,0:T(1,128)}), f32[16,1,1,32]{3,2,1,0:T(1,128)S(1)}, u32[]{:S(2)}, u32[]{:S(2)}) %all-to-all-start.3) | async-done | bytes 2080 | tf_op jit(solution)/shard_map/all_to_all | solution.py:112
  161.0 3.5 %all-to-all-start.4 = ((f32[16,1,1,32]{3,2,1,0:T(1,128)}), f32[16,1,1,32]{3,2,1,0:T(1,128)S(1)}, u32[]{:S(2)}, u32[]{:S(2)}) async-start(f32[16,1,1,32]{3,2,1,0:T(1,128)} %copy.108), calls=%async_computation.4 | async-start | bytes 16384 | tf_op jit(solution)/shard_map/all_to_all | solution.py:111
  165.3 5.6 %all-to-all-done.4 = f32[16,1,1,32]{3,2,1,0:T(1,128)S(1)} async-done(((f32[16,1,1,32]{3,2,1,0:T(1,128)}), f32[16,1,1,32]{3,2,1,0:T(1,128)S(1)}, u32[]{:S(2)}, u32[]{:S(2)}) %all-to-all-start.4) | async-done | bytes 2080 | tf_op jit(solution)/shard_map/all_to_all | solution.py:111
  170.9 3.5 %all-to-all-start.6 = ((f32[16,1,1,32]{3,2,1,0:T(1,128)}), f32[16,1,1,32]{3,2,1,0:T(1,128)S(1)}, u32[]{:S(2)}, u32[]{:S(2)}) async-start(f32[16,1,1,32]{3,2,1,0:T(1,128)} %copy.113), calls=%async_computation.6 | async-start | bytes 16384 | tf_op jit(solution)/shard_map/all_to_all | solution.py:112
  175.1 5.6 %all-to-all-done.6 = f32[16,1,1,32]{3,2,1,0:T(1,128)S(1)} async-done(((f32[16,1,1,32]{3,2,1,0:T(1,128)}), f32[16,1,1,32]{3,2,1,0:T(1,128)S(1)}, u32[]{:S(2)}, u32[]{:S(2)}) %all-to-all-start.6) | async-done | bytes 2080 | tf_op jit(solution)/shard_map/all_to_all | solution.py:112
  181.3 3.5 %all-to-all-start.7 = ((f32[16,1,1,32]{3,2,1,0:T(1,128)}), f32[16,1,1,32]{3,2,1,0:T(1,128)S(1)}, u32[]{:S(2)}, u32[]{:S(2)}) async-start(f32[16,1,1,32]{3,2,1,0:T(1,128)} %copy.114), calls=%async_computation.7 | async-start | bytes 16384 | tf_op jit(solution)/shard_map/all_to_all | solution.py:111
  185.8 6.9 %reshape.1699 = bf16[4096,4,128]{2,1,0:T(4,128)(2,1)} reshape(bf16[1,4096,512]{2,1,0:T(8,128)(2,1)} %param.24) | data formatting | bytes 8388608 | tf_op jit(solution)/shard_map/reshape.180
  192.7 6.0 %all-to-all-start.9 = ((f32[16,1,1,32]{3,2,1,0:T(1,128)}), f32[16,1,1,32]{3,2,1,0:T(1,128)S(1)}, u32[]{:S(2)}, u32[]{:S(2)}) async-start(f32[16,1,1,32]{3,2,1,0:T(1,128)} %copy.119), calls=%async_computation.9 | async-start | bytes 16384 | tf_op jit(solution)/shard_map/all_to_all | solution.py:112
  198.7 3.0 %fusion.3 = f32[4,4,8,128]{3,2,1,0:T(8,128)S(1)} fusion(bf16[4096,4,128,1]{2,1,0,3:T(4,128)(2,1)} %bitcast.285, f32[1,4,4,8,4096]{4,3,1,2,0:T(8,128)S(1)} %get-tuple-element.117, f32[4,4,8]{2,0,1:T(4,128)S(1)} %max.48), kind=kOutput, calls=%fused_computation.4 | convolution fusion | flops 135266304 | bytes 6357504 | tf_op jit(solution)/shard_map/rtkgp,rpkd->rtkgd/dot_general | solution.py:148
  202.5 2.6 all-to-all-done.9
  205.7 3.5 %all-to-all-start.10 = ((f32[16,1,1,32]{3,2,1,0:T(1,128)}), f32[16,1,1,32]{3,2,1,0:T(1,128)S(1)}, u32[]{:S(2)}, u32[]{:S(2)}) async-start(f32[16,1,1,32]{3,2,1,0:T(1,128)} %copy.120), calls=%async_computation.10 | async-start | bytes 16384 | tf_op jit(solution)/shard_map/all_to_all | solution.py:111
  209.6 0.8 copy.104
  210.4 5.1 %all-to-all-done.10 = f32[16,1,1,32]{3,2,1,0:T(1,128)S(1)} async-done(((f32[16,1,1,32]{3,2,1,0:T(1,128)}), f32[16,1,1,32]{3,2,1,0:T(1,128)S(1)}, u32[]{:S(2)}, u32[]{:S(2)}) %all-to-all-start.10) | async-done | bytes 2080 | tf_op jit(solution)/shard_map/all_to_all | solution.py:111
  215.5 3.5 %all-to-all-start.2 = ((f32[16,1,1,4096]{3,1,2,0:T(1,128)}), f32[16,1,1,4096]{3,1,2,0:T(1,128)S(1)}, u32[]{:S(2)}, u32[]{:S(2)}) async-start(f32[16,1,1,4096]{3,1,2,0:T(1,128)} %bitcast.19), calls=%async_computation.2 | async-start | bytes 524288 | tf_op jit(solution)/shard_map/all_to_all | solution.py:110
  219.1 0.8 copy.110
  219.9 0.8 copy.116
  220.7 0.8 copy.122
  222.1 7.0 %all-to-all-done.2 = f32[16,1,1,4096]{3,1,2,0:T(1,128)S(1)} async-done(((f32[16,1,1,4096]{3,1,2,0:T(1,128)}), f32[16,1,1,4096]{3,1,2,0:T(1,128)S(1)}, u32[]{:S(2)}, u32[]{:S(2)}) %all-to-all-start.2) | async-done | bytes 262176 | tf_op jit(solution)/shard_map/all_to_all | solution.py:110
  229.1 3.5 %all-to-all-start.5 = ((f32[16,1,1,4096]{3,1,2,0:T(1,128)}), f32[16,1,1,4096]{3,1,2,0:T(1,128)S(1)}, u32[]{:S(2)}, u32[]{:S(2)}) async-start(f32[16,1,1,4096]{3,1,2,0:T(1,128)} %bitcast.35), calls=%async_computation.5 | async-start | bytes 524288 | tf_op jit(solution)/shard_map/all_to_all | solution.py:110
  233.4 9.3 %all-to-all-done.5 = f32[16,1,1,4096]{3,1,2,0:T(1,128)S(1)} async-done(((f32[16,1,1,4096]{3,1,2,0:T(1,128)}), f32[16,1,1,4096]{3,1,2,0:T(1,128)S(1)}, u32[]{:S(2)}, u32[]{:S(2)}) %all-to-all-start.5) | async-done | bytes 262176 | tf_op jit(solution)/shard_map/all_to_all | solution.py:110
  242.6 3.5 %all-to-all-start.8 = ((f32[16,1,1,4096]{3,1,2,0:T(1,128)}), f32[16,1,1,4096]{3,1,2,0:T(1,128)S(1)}, u32[]{:S(2)}, u32[]{:S(2)}) async-start(f32[16,1,1,4096]{3,1,2,0:T(1,128)} %bitcast.50), calls=%async_computation.8 | async-start | bytes 524288 | tf_op jit(solution)/shard_map/all_to_all | solution.py:110
  247.6 8.6 %all-to-all-done.8 = f32[16,1,1,4096]{3,1,2,0:T(1,128)S(1)} async-done(((f32[16,1,1,4096]{3,1,2,0:T(1,128)}), f32[16,1,1,4096]{3,1,2,0:T(1,128)S(1)}, u32[]{:S(2)}, u32[]{:S(2)}) %all-to-all-start.8) | async-done | bytes 262176 | tf_op jit(solution)/shard_map/all_to_all | solution.py:110
  256.2 3.5 %all-to-all-start.11 = ((f32[16,1,1,4096]{3,1,2,0:T(1,128)}), f32[16,1,1,4096]{3,1,2,0:T(1,128)S(1)}, u32[]{:S(2)}, u32[]{:S(2)}) async-start(f32[16,1,1,4096]{3,1,2,0:T(1,128)} %bitcast.65), calls=%async_computation.11 | async-start | bytes 524288 | tf_op jit(solution)/shard_map/all_to_all | solution.py:110
  261.0 8.7 %all-to-all-done.11 = f32[16,1,1,4096]{3,1,2,0:T(1,128)S(1)} async-done(((f32[16,1,1,4096]{3,1,2,0:T(1,128)}), f32[16,1,1,4096]{3,1,2,0:T(1,128)S(1)}, u32[]{:S(2)}, u32[]{:S(2)}) %all-to-all-start.11) | async-done | bytes 262176 | tf_op jit(solution)/shard_map/all_to_all | solution.py:110
  (113 shorter events, 15.2 us)
Async XLA Ops:
  0.0 27.7 %copy-start = (bf16[1920,512]{1,0:T(8,128)(2,1)S(1)}, bf16[1920,512]{1,0:T(8,128)(2,1)}, u32[]{:S(2)}) copy-start(bf16[1920,512]{1,0:T(8,128)(2,1)} %param.16) | copy-start | bytes 5898244
  2.4 0.5 copy-start.13
  2.4 0.6 copy-start.15
  36.1 3.7 %copy-start.22 = (s32[15]{0:T(128)S(1)}, s32[15]{0:T(128)}, u32[]{:S(2)}) copy-start(s32[15]{0:T(128)} %param.17) | copy-start | bytes 184
  36.1 3.8 %copy-start.19 = (s32[64]{0:T(128)S(1)}, s32[64]{0:T(128)}, u32[]{:S(2)}) copy-start(s32[64]{0:T(128)} %constant.146.clone) | copy-start | bytes 772
  36.1 3.8 %copy-start.20 = (s32[64]{0:T(128)S(1)}, s32[64]{0:T(128)}, u32[]{:S(2)}) copy-start(s32[64]{0:T(128)} %constant.147.clone) | copy-start | bytes 772
  49.8 1.3 copy-start.2
  51.1 1.9 copy-start.4
  51.1 7.0 %copy-start.21 = (bf16[512,512]{1,0:T(8,128)(2,1)S(1)}, bf16[512,512]{1,0:T(8,128)(2,1)}, u32[]{:S(2)}) copy-start(bf16[512,512]{1,0:T(8,128)(2,1)} %param.19) | copy-start | bytes 1572868
  54.4 86.0 %all-to-all-start = ((f32[16,1,1,32]{3,2,1,0:T(1,128)}), f32[16,1,1,32]{3,2,1,0:T(1,128)S(1)}, u32[]{:S(2)}, u32[]{:S(2)}) async-start(f32[16,1,1,32]{3,2,1,0:T(1,128)} %copy.101), calls=%async_computation | async-start | bytes 16384 | tf_op jit(solution)/shard_map/all_to_all | solution.py:112
  58.1 2.1 copy-start.5
  59.4 1.7 copy-start.23
  59.4 24.6 %copy-start.3 = (bf16[1920,4,128,1]{2,0,3,1:T(8,128)(2,1)S(1)}, bf16[1920,4,128,1]{2,0,3,1:T(8,128)(2,1)}, u32[]{:S(2)}) copy-start(bf16[1920,4,128,1]{2,0,3,1:T(8,128)(2,1)} %copy-done.2) | copy-start | bytes 5898244
  84.8 1.5 copy-start.24
  86.4 20.6 %copy-start.11 = (f32[16,4,8]{0,2,1:T(8,128)}, f32[16,4,8]{0,2,1:T(8,128)S(1)}, u32[]{:S(2)}) copy-start(f32[16,4,8]{0,2,1:T(8,128)S(1)} %fusion.13) | copy-start | bytes 6148
  107.0 1.5 copy-start.25
  130.4 1.5 copy-start.26
  140.4 7.6 %copy-start.12 = (f32[16,4,8]{0,2,1:T(8,128)S(1)}, f32[16,4,8]{0,2,1:T(8,128)}, u32[]{:S(2)}) copy-start(f32[16,4,8]{0,2,1:T(8,128)} %copy-done.11) | copy-start | bytes 6148
  140.4 14.3 %copy-start.17 = (bf16[1,4,512]{2,1,0:T(4,128)(2,1)S(1)}, bf16[1,4,512]{2,1,0:T(4,128)(2,1)}, u32[]{:S(2)}) copy-start(bf16[1,4,512]{2,1,0:T(4,128)(2,1)} %param.21) | copy-start | bytes 12292
  140.4 24.1 %copy-start.14 = (f32[4,64]{1,0:T(4,128)S(1)}, f32[4,64]{1,0:T(4,128)}, u32[]{:S(2)}) copy-start(f32[4,64]{1,0:T(4,128)} %copy-done.13) | copy-start | bytes 3076
  140.4 24.1 %copy-start.16 = (f32[4,64]{1,0:T(4,128)S(1)}, f32[4,64]{1,0:T(4,128)}, u32[]{:S(2)}) copy-start(f32[4,64]{1,0:T(4,128)} %copy-done.15) | copy-start | bytes 3076
  140.4 10.2 %all-to-all-start.1 = ((f32[16,1,1,32]{3,2,1,0:T(1,128)}), f32[16,1,1,32]{3,2,1,0:T(1,128)S(1)}, u32[]{:S(2)}, u32[]{:S(2)}) async-start(f32[16,1,1,32]{3,2,1,0:T(1,128)} %copy.102), calls=%async_computation.1 | async-start | bytes 16384 | tf_op jit(solution)/shard_map/all_to_all | solution.py:111
  150.6 10.4 %all-to-all-start.3 = ((f32[16,1,1,32]{3,2,1,0:T(1,128)}), f32[16,1,1,32]{3,2,1,0:T(1,128)S(1)}, u32[]{:S(2)}, u32[]{:S(2)}) async-start(f32[16,1,1,32]{3,2,1,0:T(1,128)} %copy.107), calls=%async_computation.3 | async-start | bytes 16384 | tf_op jit(solution)/shard_map/all_to_all | solution.py:112
  161.0 23.7 %copy-start.6 = (f32[16,1,1,32]{3,2,1,0:T(1,128)}, f32[16,1,1,32]{3,2,1,0:T(1,128)S(1)}, u32[]{:S(2)}) copy-start(f32[16,1,1,32]{3,2,1,0:T(1,128)S(1)} %all-to-all-done.3) | copy-start | bytes 6148
  161.0 9.9 %all-to-all-start.4 = ((f32[16,1,1,32]{3,2,1,0:T(1,128)}), f32[16,1,1,32]{3,2,1,0:T(1,128)S(1)}, u32[]{:S(2)}, u32[]{:S(2)}) async-start(f32[16,1,1,32]{3,2,1,0:T(1,128)} %copy.108), calls=%async_computation.4 | async-start | bytes 16384 | tf_op jit(solution)/shard_map/all_to_all | solution.py:111
  170.9 9.8 %all-to-all-start.6 = ((f32[16,1,1,32]{3,2,1,0:T(1,128)}), f32[16,1,1,32]{3,2,1,0:T(1,128)S(1)}, u32[]{:S(2)}, u32[]{:S(2)}) async-start(f32[16,1,1,32]{3,2,1,0:T(1,128)} %copy.113), calls=%async_computation.6 | async-start | bytes 16384 | tf_op jit(solution)/shard_map/all_to_all | solution.py:112
  180.7 0.6 copy-start.8
  181.3 11.5 %all-to-all-start.7 = ((f32[16,1,1,32]{3,2,1,0:T(1,128)}), f32[16,1,1,32]{3,2,1,0:T(1,128)S(1)}, u32[]{:S(2)}, u32[]{:S(2)}) async-start(f32[16,1,1,32]{3,2,1,0:T(1,128)} %copy.114), calls=%async_computation.7 | async-start | bytes 16384 | tf_op jit(solution)/shard_map/all_to_all | solution.py:111
  192.7 12.3 %all-to-all-start.9 = ((f32[16,1,1,32]{3,2,1,0:T(1,128)}), f32[16,1,1,32]{3,2,1,0:T(1,128)S(1)}, u32[]{:S(2)}, u32[]{:S(2)}) async-start(f32[16,1,1,32]{3,2,1,0:T(1,128)} %copy.119), calls=%async_computation.9 | async-start | bytes 16384 | tf_op jit(solution)/shard_map/all_to_all | solution.py:112
  201.8 19.9 %copy-start.18 = (bf16[1,4,512]{2,1,0:T(4,128)(2,1)S(1)}, bf16[1,4,512]{2,1,0:T(4,128)(2,1)}, u32[]{:S(2)}) copy-start(bf16[1,4,512]{2,1,0:T(4,128)(2,1)} %param.22) | copy-start | bytes 12292
  201.8 20.3 %copy-start.7 = (f32[16,1,1,32]{3,2,1,0:T(1,128)S(1)}, f32[16,1,1,32]{3,2,1,0:T(1,128)}, u32[]{:S(2)}) copy-start(f32[16,1,1,32]{3,2,1,0:T(1,128)} %copy-done.6) | copy-start | bytes 6148
  201.8 20.3 %copy-start.9 = (f32[16,1,1,32]{3,2,1,0:T(1,128)S(1)}, f32[16,1,1,32]{3,2,1,0:T(1,128)}, u32[]{:S(2)}) copy-start(f32[16,1,1,32]{3,2,1,0:T(1,128)} %copy-done.8) | copy-start | bytes 6148
  205.1 0.6 copy-start.10
  205.7 9.9 %all-to-all-start.10 = ((f32[16,1,1,32]{3,2,1,0:T(1,128)}), f32[16,1,1,32]{3,2,1,0:T(1,128)S(1)}, u32[]{:S(2)}, u32[]{:S(2)}) async-start(f32[16,1,1,32]{3,2,1,0:T(1,128)} %copy.120), calls=%async_computation.10 | async-start | bytes 16384 | tf_op jit(solution)/shard_map/all_to_all | solution.py:111
  215.5 13.5 %all-to-all-start.2 = ((f32[16,1,1,4096]{3,1,2,0:T(1,128)}), f32[16,1,1,4096]{3,1,2,0:T(1,128)S(1)}, u32[]{:S(2)}, u32[]{:S(2)}) async-start(f32[16,1,1,4096]{3,1,2,0:T(1,128)} %bitcast.19), calls=%async_computation.2 | async-start | bytes 524288 | tf_op jit(solution)/shard_map/all_to_all | solution.py:110
  219.1 52.2 %copy-start.1 = (bf16[1920,512]{1,0:T(8,128)(2,1)S(1)}, bf16[1920,512]{1,0:T(8,128)(2,1)}, u32[]{:S(2)}) copy-start(bf16[1920,512]{1,0:T(8,128)(2,1)} %param.16) | copy-start | bytes 5898244
  229.1 13.5 %all-to-all-start.5 = ((f32[16,1,1,4096]{3,1,2,0:T(1,128)}), f32[16,1,1,4096]{3,1,2,0:T(1,128)S(1)}, u32[]{:S(2)}, u32[]{:S(2)}) async-start(f32[16,1,1,4096]{3,1,2,0:T(1,128)} %bitcast.35), calls=%async_computation.5 | async-start | bytes 524288 | tf_op jit(solution)/shard_map/all_to_all | solution.py:110
  242.6 13.5 %all-to-all-start.8 = ((f32[16,1,1,4096]{3,1,2,0:T(1,128)}), f32[16,1,1,4096]{3,1,2,0:T(1,128)S(1)}, u32[]{:S(2)}, u32[]{:S(2)}) async-start(f32[16,1,1,4096]{3,1,2,0:T(1,128)} %bitcast.50), calls=%async_computation.8 | async-start | bytes 524288 | tf_op jit(solution)/shard_map/all_to_all | solution.py:110
  256.2 13.5 %all-to-all-start.11 = ((f32[16,1,1,4096]{3,1,2,0:T(1,128)}), f32[16,1,1,4096]{3,1,2,0:T(1,128)S(1)}, u32[]{:S(2)}, u32[]{:S(2)}) async-start(f32[16,1,1,4096]{3,1,2,0:T(1,128)} %bitcast.65), calls=%async_computation.11 | async-start | bytes 524288 | tf_op jit(solution)/shard_map/all_to_all | solution.py:110
where the time goes:
time: 273 us; the launch traced here: 271 us
  blocking collectives  83.6 us (31%)
  waiting for transfers between devices  59.9 us (22%)
  starting transfers between devices  45.6 us (17%)
  local copies, waits for them, and re-layouts  40.9 us (15%)
  other arithmetic  22.1 us (8%)
  matrix products  17.6 us (6%)
    all_gather x4, blocking collectives, prefix_attention(): whole = lax.all_gather(selected, 'seq', axis=0, tiled=True)  83.6 us
    all_to_all x4, waiting for transfers between devices, prefix_attention(): lax.all_to_all(parts[:, None], 'seq', split_axis=0, concat_axis=1, tiled=...  33.5 us
    all_to_all x4, starting transfers between devices, prefix_attention(): lax.all_to_all(totals[:, None], 'seq', split_axis=0, concat_axis=1, tiled...  17.2 us
    unnamed x61, local copies, waits for them, and re-layouts  14.6 us
    all_to_all x4, starting transfers between devices, prefix_attention(): lax.all_to_all(peaks[:, None], 'seq', split_axis=0, concat_axis=1, tiled=...  14.3 us
    all_to_all x4, starting transfers between devices, prefix_attention(): lax.all_to_all(parts[:, None], 'seq', split_axis=0, concat_axis=1, tiled=...  14.1 us
    another operation x2, local copies, waits for them, and re-layouts  13.9 us
    all_to_all x4, waiting for transfers between devices, prefix_attention(): lax.all_to_all(totals[:, None], 'seq', split_axis=0, concat_axis=1, tiled...  13.8 us
  transfers between devices with their start and end apart: 12, of which 10 were waited for; matrix products, arithmetic and copies ran while one was open for 17% of the time, Pallas kernels for 0%

commit v1 on v0

--- a/solution.py
+++ b/solution.py
@@ -1,3 +1,4 @@
+import functools
 import math
 import jax
 import jax.numpy as jnp
@@ -11,6 +12,18 @@
 BLK = 128
 STEPS = 4
 SUF = 4096
+
+
+def _store_spans(local_values, axis_key):
+    return jnp.concatenate(
+        lax.all_to_all(
+            jnp.stack(jnp.split(local_values, lax.axis_size(axis_key), 0), 0), axis_key, 0, 0
+        ),
+        1,
+    )
+
+
+produce_pieces_all_by_axis = functools.partial(_store_spans, axis_key="seq")
 
 
 def phase_table(half):
@@ -108,7 +121,7 @@
         totals = totals.reshape(count, width, QH)
         got_parts, got_peaks, got_totals = (
             lax.all_to_all(parts[:, None], "seq", split_axis=0, concat_axis=1, tiled=True),
-            lax.all_to_all(peaks[:, None], "seq", split_axis=0, concat_axis=1, tiled=True),
+            produce_pieces_all_by_axis(peaks[:, None]),
             lax.all_to_all(totals[:, None], "seq", split_axis=0, concat_axis=1, tiled=True),
         )
         highest = jnp.max(got_peaks, 1)

time: 273 us -> 336 us (1.23)
  local copies, waits for them, and re-layouts: 40.9 us -> 75.7 us
  matrix products: 17.6 us -> 34.4 us
  other arithmetic: 22.1 us -> 33.1 us
    unnamed x61 -> x153, local copies, waits for them, and re-layouts: 14.6 us -> 33.2 us
    another operation x6 -> x70, local copies, waits for them, and re-layouts: 16.5 us -> 31.5 us  [the longest x68 17.7 us: _store_spans(): jnp.stack(jnp.split(local_values, lax.axis_size(axis_key), 0), 0)]
    reduce_sum x4, other arithmetic: 3.1 us -> 12 us  [shard_part(): total = jnp.sum(expo, -1)]
    dot_general x4, matrix products: 3.18 us -> 12 us  [shard_part(): jnp.einsum('rtkgd,pkd->rtkgp', split, keys, preferred_element_type=jnp.fl...]
    dot_general x4, matrix products: 3.38 us -> 8.19 us  [shard_part(): jnp.einsum('rtkgp,pkd->rtkgd', expo.astype(jnp.bfloat16), values, preferr...]
  transfers between devices with their start and end apart: 12 -> 12, of which waited for: 10 -> 10; matrix products, arithmetic and copies ran while one was open for 17% -> 31% of each run, Pallas kernels for 0% -> 0%
where the time goes in v1:
time: 336 us; the launch traced here: 334 us
  blocking collectives  83.9 us (25%)
  local copies, waits for them, and re-layouts  75.7 us (23%)
  waiting for transfers between devices  60.7 us (18%)
  starting transfers between devices  45 us (13%)
  matrix products  34.4 us (10%)
  other arithmetic  33.1 us (10%)
    all_gather x4, blocking collectives, prefix_attention(): whole = lax.all_gather(selected, 'seq', axis=0, tiled=True)  83.9 us
    all_to_all x4, waiting for transfers between devices, prefix_attention(): lax.all_to_all(parts[:, None], 'seq', split_axis=0, concat_axis=1, tiled=...  33.5 us
    unnamed x153, local copies, waits for them, and re-layouts  33.2 us
    another operation x68, local copies, waits for them, and re-layouts, _store_spans(): jnp.stack(jnp.split(local_values, lax.axis_size(axis_key), 0), 0)  17.7 us
    all_to_all x4, starting transfers between devices, _store_spans(): lax.all_to_all(jnp.stack(jnp.split(local_values, lax.axis_size(axis_key),...  16.5 us
    all_to_all x4, waiting for transfers between devices, prefix_attention(): lax.all_to_all(totals[:, None], 'seq', split_axis=0, concat_axis=1, tiled...  15.1 us
    all_to_all x4, starting transfers between devices, prefix_attention(): lax.all_to_all(totals[:, None], 'seq', split_axis=0, concat_axis=1, tiled...  14.4 us
    all_to_all x4, starting transfers between devices, prefix_attention(): lax.all_to_all(parts[:, None], 'seq', split_axis=0, concat_axis=1, tiled=...  14.1 us
  transfers between devices with their start and end apart: 12, of which 10 were waited for; matrix products, arithmetic and copies ran while one was open for 31% of the time, Pallas kernels for 0%

profile of v1, /device:TPU:0, one launch (start us, length us, event | category | flops | bytes accessed | tf_op | source)
XLA Modules:
  0.0 334.4 jit_solution(5839990708131028572)
XLA Ops:
  0.8 0.8 convert_bitcast_fusion
  1.6 0.8 fusion.115
  2.7 23.8 %all_gather.12 = bf16[16,1,4096]{2,1,0:T(2,128)(2,1)S(1)} all-gather(bf16[1,1,4096]{2,1,0:T(2,128)(2,1)S(1)} %get-tuple-element.162), channel_id=1, replica_groups=mesh['parts'=2,'seq'=16] {'seq'}, dimensions={0}, use_global_device_ids=true | all-gather | bytes 139264 | tf_op jit(solution)/shard_map/all_gather | solution.py:114
  26.5 0.7 reduce.40
  27.2 2.4 fusion.127
  29.6 2.3 fusion.123
  32.0 3.7 %copy.219 = f32[1920,4,64]{2,0,1:T(8,128)} copy(f32[1920,4,64]{0,2,1:T(8,128)} %get-tuple-element.159) | data formatting | bytes 3932160
  35.6 3.7 %copy.220 = f32[1920,4,64]{2,0,1:T(8,128)} copy(f32[1920,4,64]{0,2,1:T(8,128)} %get-tuple-element.158) | data formatting | bytes 3932160
  39.4 4.3 %fusion.77 = (f32[1920,64]{1,0:T(8,128)S(1)}, f32[1920,64]{1,0:T(8,128)S(1)}) fusion(s32[64]{0:T(128)S(1)} %copy-done.18, s32[64]{0:T(128)S(1)} %copy-done.17, s32[1920]{0:T(1024)S(1)} %fusion.96), kind=kLoop, calls=%fused_computation.80 | loop fusion | flops 3440640 | bytes 991232 | tf_op jit(solution)/shard_map/cos | solution.py:44
  43.8 4.5 %subtract_convert_fusion = (bf16[1920,4,64]{2,0,1:T(8,128)(2,1)S(1)}, bf16[1920,4,64]{2,0,1:T(8,128)(2,1)S(1)}) fusion(f32[1920,4,64]{2,0,1:T(8,128)} %copy.220, f32[1920,4,64]{2,0,1:T(8,128)} %copy.219, f32[1920,64]{1,0:T(8,128)S(1)} %get-tuple-element.169, f32[1920,64]{1,0:T(8,128)S(1)} %get-tuple-element.168), kind=kLoop, calls=%fused_computation.20 | loop fusion | flops 3932160 | bytes 6881280 | tf_op jit(solution)/shard_map/convert.12
  48.2 1.1 maximum_bitcast_fusion
  49.3 2.6 bitcast_reduce_fusion.3
  62.2 3.6 %all-to-all-start.1 = ((f32[16,1,1,1,32]{4,3,2,1,0:T(1,128)}), f32[16,1,1,1,32]{4,3,2,1,0:T(1,128)S(1)}, u32[]{:S(2)}, u32[]{:S(2)}) async-start(f32[16,1,1,1,32]{4,3,2,1,0:T(1,128)} %constant_dynamic-update-slice_fusion), calls=%async_computation.1 | async-start | bytes 16384 | tf_op jit(solution)/shard_map/all_to_all | solution.py:19
  66.3 2.9 fusion.11
  69.2 2.6 convolution_convert_fusion
  71.8 22.2 %all_gather.13 = bf16[16,1,4096]{2,1,0:T(2,128)(2,1)S(1)} all-gather(bf16[1,1,4096]{2,1,0:T(2,128)(2,1)S(1)} %get-tuple-element.165), channel_id=1, replica_groups=mesh['parts'=2,'seq'=16] {'seq'}, dimensions={0}, use_global_device_ids=true | all-gather | bytes 139264 | tf_op jit(solution)/shard_map/all_gather | solution.py:114
  94.0 0.7 reduce.57
  94.8 4.2 %bitcast_reduce_fusion.2 = (f32[16,4,8]{0,2,1:T(8,128)S(1)}, f32[4,1920,16,8]{1,2,3,0:T(8,128)}) fusion(bf16[1920,4,128,1]{2,0,3,1:T(8,128)(2,1)} %copy-done.2, bf16[16,4,8,128]{3,2,1,0:T(8,128)(2,1)S(1)} %bitcast.289), kind=kOutput, calls=%fused_computation.14 | convolution fusion | flops 253623808 | bytes 6031360 | tf_op jit(solution)/shard_map/while/body/eval_jaxpr/rtkgd,pkd->rtkgp/dot_general | solution.py:94
  103.7 3.1 fusion.13
  107.0 2.5 fusion.64
  110.1 0.8 fusion.61
  110.9 18.2 %all_gather.14 = bf16[16,1,4096]{2,1,0:T(2,128)(2,1)S(1)} all-gather(bf16[1,1,4096]{2,1,0:T(2,128)(2,1)S(1)} %get-tuple-element.164), channel_id=1, replica_groups=mesh['parts'=2,'seq'=16] {'seq'}, dimensions={0}, use_global_device_ids=true | all-gather | bytes 139264 | tf_op jit(solution)/shard_map/all_gather | solution.py:114
  129.1 0.7 reduce.74
  129.9 2.6 bitcast_reduce_fusion.1
  142.2 3.0 fusion.15
  145.5 2.4 fusion.58
  147.9 19.7 %all_gather.15 = bf16[16,1,4096]{2,1,0:T(2,128)(2,1)S(1)} all-gather(bf16[1,1,4096]{2,1,0:T(2,128)(2,1)S(1)} %get-tuple-element.163), channel_id=1, replica_groups=mesh['parts'=2,'seq'=16] {'seq'}, dimensions={0}, use_global_device_ids=true | all-gather | bytes 139264 | tf_op jit(solution)/shard_map/all_gather | solution.py:114
  167.6 0.7 reduce.91
  168.4 2.6 bitcast_reduce_fusion
  172.7 3.1 fusion.17
  176.0 2.4 fusion.55
  178.7 6.9 %reshape.1959 = bf16[4096,4,128]{2,1,0:T(4,128)(2,1)} reshape(bf16[1,4096,512]{2,1,0:T(8,128)(2,1)} %param.23) | data formatting | bytes 8388608 | tf_op jit(solution)/shard_map/reshape.285
  199.0 5.1 %fusion.125 = (f32[4,4,8]{2,0,1:T(4,128)S(1)}, f32[1,4,4,8,4096]{4,3,1,2,0:T(8,128)}) fusion(bf16[4096,4,128,1]{2,1,0,3:T(4,128)(2,1)} %bitcast.281, pred[4096]{0:T(1024)(128)(4,1)S(1)} %iota_compare_fusion, bf16[4,4,8,64]{3,2,1,0:T(8,128)(2,1)S(1)} %bitcast.297, bf16[4,4,8,64]{3,2,1,0:T(8,128)(2,1)S(1)} %bitcast.295), kind=kOutput, calls=%fused_computation.295 | convolution fusion | flops 135856000 | bytes 6328832 | tf_op jit(solution)/shard_map/rtkgd,rpkd->rtkgp/dot_general | solution.py:144
  205.6 3.5 %all-to-all-start = ((f32[16,1,1,32]{3,2,1,0:T(1,128)}), f32[16,1,1,32]{3,2,1,0:T(1,128)S(1)}, u32[]{:S(2)}, u32[]{:S(2)}) async-start(f32[16,1,1,32]{3,2,1,0:T(1,128)} %copy.169), calls=%async_computation | async-start | bytes 16384 | tf_op jit(solution)/shard_map/all_to_all | solution.py:125
  209.7 5.8 %all-to-all-done = f32[16,1,1,32]{3,2,1,0:T(1,128)S(1)} async-done(((f32[16,1,1,32]{3,2,1,0:T(1,128)}), f32[16,1,1,32]{3,2,1,0:T(1,128)S(1)}, u32[]{:S(2)}, u32[]{:S(2)}) %all-to-all-start) | async-done | bytes 2080 | tf_op jit(solution)/shard_map/all_to_all | solution.py:125
  215.5 3.4 %all-to-all-start.4 = ((f32[16,1,1,1,32]{4,3,2,1,0:T(1,128)}), f32[16,1,1,1,32]{4,3,2,1,0:T(1,128)S(1)}, u32[]{:S(2)}, u32[]{:S(2)}) async-start(f32[16,1,1,1,32]{4,3,2,1,0:T(1,128)} %constant_dynamic-update-slice_fusion.16), calls=%async_computation.4 | async-start | bytes 16384 | tf_op jit(solution)/shard_map/all_to_all | solution.py:19
  220.3 5.0 %all-to-all-done.4 = f32[16,1,1,1,32]{4,3,2,1,0:T(1,128)S(1)} async-done(((f32[16,1,1,1,32]{4,3,2,1,0:T(1,128)}), f32[16,1,1,1,32]{4,3,2,1,0:T(1,128)S(1)}, u32[]{:S(2)}, u32[]{:S(2)}) %all-to-all-start.4) | async-done | bytes 2080 | tf_op jit(solution)/shard_map/all_to_all | solution.py:19
  225.3 3.5 %all-to-all-start.3 = ((f32[16,1,1,32]{3,2,1,0:T(1,128)}), f32[16,1,1,32]{3,2,1,0:T(1,128)S(1)}, u32[]{:S(2)}, u32[]{:S(2)}) async-start(f32[16,1,1,32]{3,2,1,0:T(1,128)} %copy.174), calls=%async_computation.3 | async-start | bytes 16384 | tf_op jit(solution)/shard_map/all_to_all | solution.py:125
  229.4 5.8 %all-to-all-done.3 = f32[16,1,1,32]{3,2,1,0:T(1,128)S(1)} async-done(((f32[16,1,1,32]{3,2,1,0:T(1,128)}), f32[16,1,1,32]{3,2,1,0:T(1,128)S(1)}, u32[]{:S(2)}, u32[]{:S(2)}) %all-to-all-start.3) | async-done | bytes 2080 | tf_op jit(solution)/shard_map/all_to_all | solution.py:125
  235.2 3.4 %all-to-all-start.7 = ((f32[16,1,1,1,32]{4,3,2,1,0:T(1,128)}), f32[16,1,1,1,32]{4,3,2,1,0:T(1,128)S(1)}, u32[]{:S(2)}, u32[]{:S(2)}) async-start(f32[16,1,1,1,32]{4,3,2,1,0:T(1,128)} %copy-done.14), calls=%async_computation.7 | async-start | bytes 16384 | tf_op jit(solution)/shard_map/all_to_all | solution.py:19
  239.9 5.1 %all-to-all-done.7 = f32[16,1,1,1,32]{4,3,2,1,0:T(1,128)S(1)} async-done(((f32[16,1,1,1,32]{4,3,2,1,0:T(1,128)}), f32[16,1,1,1,32]{4,3,2,1,0:T(1,128)S(1)}, u32[]{:S(2)}, u32[]{:S(2)}) %all-to-all-start.7) | async-done | bytes 2080 | tf_op jit(solution)/shard_map/all_to_all | solution.py:19
  245.0 3.5 %all-to-all-start.6 = ((f32[16,1,1,32]{3,2,1,0:T(1,128)}), f32[16,1,1,32]{3,2,1,0:T(1,128)S(1)}, u32[]{:S(2)}, u32[]{:S(2)}) async-start(f32[16,1,1,32]{3,2,1,0:T(1,128)} %copy.179), calls=%async_computation.6 | async-start | bytes 16384 | tf_op jit(solution)/shard_map/all_to_all | solution.py:125
  249.0 6.9 %reshape.1963 = bf16[4096,4,128]{2,1,0:T(4,128)(2,1)} reshape(bf16[1,4096,512]{2,1,0:T(8,128)(2,1)} %param.24) | data formatting | bytes 8388608 | tf_op jit(solution)/shard_map/reshape.300
  256.0 6.0 %all-to-all-start.10 = ((f32[16,1,1,1,32]{4,3,2,1,0:T(1,128)}), f32[16,1,1,1,32]{4,3,2,1,0:T(1,128)S(1)}, u32[]{:S(2)}, u32[]{:S(2)}) async-start(f32[16,1,1,1,32]{4,3,2,1,0:T(1,128)} %constant_dynamic-update-slice_fusion.48), calls=%async_computation.10 | async-start | bytes 16384 | tf_op jit(solution)/shard_map/all_to_all | solution.py:19
  262.0 3.7 %fusion.3 = f32[4,4,8,128]{3,2,1,0:T(8,128)S(1)} fusion(bf16[4096,4,128,1]{2,1,0,3:T(4,128)(2,1)} %bitcast.282, f32[1,4,4,8,4096]{4,3,1,2,0:T(8,128)} %get-tuple-element.181, f32[4,4,8]{2,0,1:T(4,128)S(1)} %max.48), kind=kOutput, calls=%fused_computation.4 | convolution fusion | flops 135266304 | bytes 6357504 | tf_op jit(solution)/shard_map/rtkgp,rpkd->rtkgd/dot_general | solution.py:161
  266.3 2.0 all-to-all-done.10
  268.4 4.0 %all-to-all-start.9 = ((f32[16,1,1,32]{3,2,1,0:T(1,128)}), f32[16,1,1,32]{3,2,1,0:T(1,128)S(1)}, u32[]{:S(2)}, u32[]{:S(2)}) async-start(f32[16,1,1,32]{3,2,1,0:T(1,128)} %copy.184), calls=%async_computation.9 | async-start | bytes 16384 | tf_op jit(solution)/shard_map/all_to_all | solution.py:125
  272.4 2.0 fusion.38
  274.4 0.8 copy.171
  275.2 3.5 %all-to-all-done.9 = f32[16,1,1,32]{3,2,1,0:T(1,128)S(1)} async-done(((f32[16,1,1,32]{3,2,1,0:T(1,128)}), f32[16,1,1,32]{3,2,1,0:T(1,128)S(1)}, u32[]{:S(2)}, u32[]{:S(2)}) %all-to-all-start.9) | async-done | bytes 2080 | tf_op jit(solution)/shard_map/all_to_all | solution.py:125
  278.7 3.5 %all-to-all-start.2 = ((f32[16,1,1,4096]{3,1,2,0:T(1,128)}), f32[16,1,1,4096]{3,1,2,0:T(1,128)S(1)}, u32[]{:S(2)}, u32[]{:S(2)}) async-start(f32[16,1,1,4096]{3,1,2,0:T(1,128)} %bitcast.18), calls=%async_computation.2 | async-start | bytes 524288 | tf_op jit(solution)/shard_map/all_to_all | solution.py:123
  282.3 0.8 copy.176
  283.1 0.8 copy.181
  283.9 0.8 copy.186
  285.3 7.0 %all-to-all-done.2 = f32[16,1,1,4096]{3,1,2,0:T(1,128)S(1)} async-done(((f32[16,1,1,4096]{3,1,2,0:T(1,128)}), f32[16,1,1,4096]{3,1,2,0:T(1,128)S(1)}, u32[]{:S(2)}, u32[]{:S(2)}) %all-to-all-start.2) | async-done | bytes 262176 | tf_op jit(solution)/shard_map/all_to_all | solution.py:123
  292.2 3.5 %all-to-all-start.5 = ((f32[16,1,1,4096]{3,1,2,0:T(1,128)}), f32[16,1,1,4096]{3,1,2,0:T(1,128)S(1)}, u32[]{:S(2)}, u32[]{:S(2)}) async-start(f32[16,1,1,4096]{3,1,2,0:T(1,128)} %bitcast.33), calls=%async_computation.5 | async-start | bytes 524288 | tf_op jit(solution)/shard_map/all_to_all | solution.py:123
  295.8 0.7 multiply_reduce_fusion.4
  296.5 9.3 %all-to-all-done.5 = f32[16,1,1,4096]{3,1,2,0:T(1,128)S(1)} async-done(((f32[16,1,1,4096]{3,1,2,0:T(1,128)}), f32[16,1,1,4096]{3,1,2,0:T(1,128)S(1)}, u32[]{:S(2)}, u32[]{:S(2)}) %all-to-all-start.5) | async-done | bytes 262176 | tf_op jit(solution)/shard_map/all_to_all | solution.py:123
  305.8 3.5 %all-to-all-start.8 = ((f32[16,1,1,4096]{3,1,2,0:T(1,128)}), f32[16,1,1,4096]{3,1,2,0:T(1,128)S(1)}, u32[]{:S(2)}, u32[]{:S(2)}) async-start(f32[16,1,1,4096]{3,1,2,0:T(1,128)} %bitcast.47), calls=%async_computation.8 | async-start | bytes 524288 | tf_op jit(solution)/shard_map/all_to_all | solution.py:123
  309.4 0.7 exponential_multiply_fusion.1
  310.1 0.7 exponential_multiply_fusion
  310.8 8.6 %all-to-all-done.8 = f32[16,1,1,4096]{3,1,2,0:T(1,128)S(1)} async-done(((f32[16,1,1,4096]{3,1,2,0:T(1,128)}), f32[16,1,1,4096]{3,1,2,0:T(1,128)S(1)}, u32[]{:S(2)}, u32[]{:S(2)}) %all-to-all-start.8) | async-done | bytes 262176 | tf_op jit(solution)/shard_map/all_to_all | solution.py:123
  319.3 3.5 %all-to-all-start.11 = ((f32[16,1,1,4096]{3,1,2,0:T(1,128)}), f32[16,1,1,4096]{3,1,2,0:T(1,128)S(1)}, u32[]{:S(2)}, u32[]{:S(2)}) async-start(f32[16,1,1,4096]{3,1,2,0:T(1,128)} %bitcast.61), calls=%async_computation.11 | async-start | bytes 524288 | tf_op jit(solution)/shard_map/all_to_all | solution.py:123
  324.2 8.7 %all-to-all-done.11 = f32[16,1,1,4096]{3,1,2,0:T(1,128)S(1)} async-done(((f32[16,1,1,4096]{3,1,2,0:T(1,128)}), f32[16,1,1,4096]{3,1,2,0:T(1,128)S(1)}, u32[]{:S(2)}, u32[]{:S(2)}) %all-to-all-start.11) | async-done | bytes 262176 | tf_op jit(solution)/shard_map/all_to_all | solution.py:123
  (273 shorter events, 52.1 us)
Async XLA Ops:
  0.0 27.2 %copy-start = (bf16[1920,512]{1,0:T(8,128)(2,1)S(1)}, bf16[1920,512]{1,0:T(8,128)(2,1)}, u32[]{:S(2)}) copy-start(bf16[1920,512]{1,0:T(8,128)(2,1)} %param.16) | copy-start | bytes 5898244
  35.6 3.7 %copy-start.40 = (s32[15]{0:T(128)S(1)}, s32[15]{0:T(128)}, u32[]{:S(2)}) copy-start(s32[15]{0:T(128)} %param.17) | copy-start | bytes 184
  35.6 3.8 %copy-start.17 = (s32[64]{0:T(128)S(1)}, s32[64]{0:T(128)}, u32[]{:S(2)}) copy-start(s32[64]{0:T(128)} %constant.146.clone) | copy-start | bytes 772
  35.6 3.8 %copy-start.18 = (s32[64]{0:T(128)S(1)}, s32[64]{0:T(128)}, u32[]{:S(2)}) copy-start(s32[64]{0:T(128)} %constant.147.clone) | copy-start | bytes 772
  49.3 2.6 copy-start.2
  51.9 17.3 %copy-start.39 = (bf16[512,512]{1,0:T(8,128)(2,1)S(1)}, bf16[512,512]{1,0:T(8,128)(2,1)}, u32[]{:S(2)}) copy-start(bf16[512,512]{1,0:T(8,128)(2,1)} %param.19) | copy-start | bytes 1572868
  62.2 143.5 %all-to-all-start.1 = ((f32[16,1,1,1,32]{4,3,2,1,0:T(1,128)}), f32[16,1,1,1,32]{4,3,2,1,0:T(1,128)S(1)}, u32[]{:S(2)}, u32[]{:S(2)}) async-start(f32[16,1,1,1,32]{4,3,2,1,0:T(1,128)} %constant_dynamic-update-slice_fusion), calls=%async_computation.1 | async-start | bytes 16384 | tf_op jit(solution)/shard_map/all_to_all | solution.py:19
  103.7 3.3 copy-start.4
  106.8 4.2 %copy-start.10 = (f32[16,4,8]{0,2,1:T(8,128)}, f32[16,4,8]{0,2,1:T(8,128)S(1)}, u32[]{:S(2)}) copy-start(f32[16,4,8]{0,2,1:T(8,128)S(1)} %fusion.13) | copy-start | bytes 6148
  106.8 2.8 copy-start.5
  106.8 3.3 copy-start.41
  110.1 19.8 %copy-start.3 = (bf16[1920,4,128,1]{2,0,3,1:T(8,128)(2,1)S(1)}, bf16[1920,4,128,1]{2,0,3,1:T(8,128)(2,1)}, u32[]{:S(2)}) copy-start(bf16[1920,4,128,1]{2,0,3,1:T(8,128)(2,1)} %copy-done.2) | copy-start | bytes 5898244
  142.2 3.3 copy-start.6
  145.5 25.5 %copy-start.12 = (f32[16,4,8]{0,2,1:T(8,128)}, f32[16,4,8]{0,2,1:T(8,128)S(1)}, u32[]{:S(2)}) copy-start(f32[16,4,8]{0,2,1:T(8,128)S(1)} %fusion.15) | copy-start | bytes 6148
  172.7 3.3 copy-start.7
  176.0 2.4 copy-start.15
  178.5 7.1 %copy-start.22 = (f32[1,1,1,1,32]{4,3,2,1,0:T(1,128)S(1)}, f32[1,1,1,1,32]{4,3,2,1,0:T(1,128)}, u32[]{:S(2)}) copy-start(f32[1,1,1,1,32]{4,3,2,1,0:T(1,128)} %stack.222) | copy-start | bytes 388
  178.5 7.7 %copy-start.23 = (f32[1,1,1,1,32]{4,3,2,1,0:T(1,128)S(1)}, f32[1,1,1,1,32]{4,3,2,1,0:T(1,128)}, u32[]{:S(2)}) copy-start(f32[1,1,1,1,32]{4,3,2,1,0:T(1,128)} %stack.223) | copy-start | bytes 388
  178.5 8.3 %copy-start.21 = (f32[1,1,1,1,32]{4,3,2,1,0:T(1,128)S(1)}, f32[1,1,1,1,32]{4,3,2,1,0:T(1,128)}, u32[]{:S(2)}) copy-start(f32[1,1,1,1,32]{4,3,2,1,0:T(1,128)} %stack.224) | copy-start | bytes 388
  178.5 8.8 %copy-start.20 = (f32[1,1,1,1,32]{4,3,2,1,0:T(1,128)S(1)}, f32[1,1,1,1,32]{4,3,2,1,0:T(1,128)}, u32[]{:S(2)}) copy-start(f32[1,1,1,1,32]{4,3,2,1,0:T(1,128)} %stack.225) | copy-start | bytes 388
  178.6 9.4 %copy-start.19 = (f32[1,1,1,1,32]{4,3,2,1,0:T(1,128)S(1)}, f32[1,1,1,1,32]{4,3,2,1,0:T(1,128)}, u32[]{:S(2)}) copy-start(f32[1,1,1,1,32]{4,3,2,1,0:T(1,128)} %stack.226) | copy-start | bytes 388
  178.6 15.2 %copy-start.37 = (f32[1,1,1,1,32]{4,3,2,1,0:T(1,128)S(1)}, f32[1,1,1,1,32]{4,3,2,1,0:T(1,128)}, u32[]{:S(2)}) copy-start(f32[1,1,1,1,32]{4,3,2,1,0:T(1,128)} %stack.239) | copy-start | bytes 388
  178.6 15.2 %copy-start.38 = (f32[1,1,1,1,32]{4,3,2,1,0:T(1,128)S(1)}, f32[1,1,1,1,32]{4,3,2,1,0:T(1,128)}, u32[]{:S(2)}) copy-start(f32[1,1,1,1,32]{4,3,2,1,0:T(1,128)} %stack.240) | copy-start | bytes 388
  178.6 15.2 %copy-start.36 = (f32[1,1,1,1,32]{4,3,2,1,0:T(1,128)S(1)}, f32[1,1,1,1,32]{4,3,2,1,0:T(1,128)}, u32[]{:S(2)}) copy-start(f32[1,1,1,1,32]{4,3,2,1,0:T(1,128)} %stack.241) | copy-start | bytes 388
  178.6 15.2 %copy-start.35 = (f32[1,1,1,1,32]{4,3,2,1,0:T(1,128)S(1)}, f32[1,1,1,1,32]{4,3,2,1,0:T(1,128)}, u32[]{:S(2)}) copy-start(f32[1,1,1,1,32]{4,3,2,1,0:T(1,128)} %stack.242) | copy-start | bytes 388
  178.6 15.2 %copy-start.34 = (f32[1,1,1,1,32]{4,3,2,1,0:T(1,128)S(1)}, f32[1,1,1,1,32]{4,3,2,1,0:T(1,128)}, u32[]{:S(2)}) copy-start(f32[1,1,1,1,32]{4,3,2,1,0:T(1,128)} %stack.243) | copy-start | bytes 388
  178.6 15.2 %copy-start.33 = (f32[1,1,1,1,32]{4,3,2,1,0:T(1,128)S(1)}, f32[1,1,1,1,32]{4,3,2,1,0:T(1,128)}, u32[]{:S(2)}) copy-start(f32[1,1,1,1,32]{4,3,2,1,0:T(1,128)} %stack.244) | copy-start | bytes 388
  178.6 15.2 %copy-start.32 = (f32[1,1,1,1,32]{4,3,2,1,0:T(1,128)S(1)}, f32[1,1,1,1,32]{4,3,2,1,0:T(1,128)}, u32[]{:S(2)}) copy-start(f32[1,1,1,1,32]{4,3,2,1,0:T(1,128)} %stack.245) | copy-start | bytes 388
  178.6 15.2 %copy-start.31 = (f32[1,1,1,1,32]{4,3,2,1,0:T(1,128)S(1)}, f32[1,1,1,1,32]{4,3,2,1,0:T(1,128)}, u32[]{:S(2)}) copy-start(f32[1,1,1,1,32]{4,3,2,1,0:T(1,128)} %stack.246) | copy-start | bytes 388
  178.6 15.3 %copy-start.30 = (f32[1,1,1,1,32]{4,3,2,1,0:T(1,128)S(1)}, f32[1,1,1,1,32]{4,3,2,1,0:T(1,128)}, u32[]{:S(2)}) copy-start(f32[1,1,1,1,32]{4,3,2,1,0:T(1,128)} %stack.247) | copy-start | bytes 388
  178.7 15.3 %copy-start.29 = (f32[1,1,1,1,32]{4,3,2,1,0:T(1,128)S(1)}, f32[1,1,1,1,32]{4,3,2,1,0:T(1,128)}, u32[]{:S(2)}) copy-start(f32[1,1,1,1,32]{4,3,2,1,0:T(1,128)} %stack.248) | copy-start | bytes 388
  178.7 15.3 %copy-start.28 = (f32[1,1,1,1,32]{4,3,2,1,0:T(1,128)S(1)}, f32[1,1,1,1,32]{4,3,2,1,0:T(1,128)}, u32[]{:S(2)}) copy-start(f32[1,1,1,1,32]{4,3,2,1,0:T(1,128)} %stack.249) | copy-start | bytes 388
  178.7 15.3 %copy-start.27 = (f32[1,1,1,1,32]{4,3,2,1,0:T(1,128)S(1)}, f32[1,1,1,1,32]{4,3,2,1,0:T(1,128)}, u32[]{:S(2)}) copy-start(f32[1,1,1,1,32]{4,3,2,1,0:T(1,128)} %stack.250) | copy-start | bytes 388
  178.7 15.3 %copy-start.26 = (f32[1,1,1,1,32]{4,3,2,1,0:T(1,128)S(1)}, f32[1,1,1,1,32]{4,3,2,1,0:T(1,128)}, u32[]{:S(2)}) copy-start(f32[1,1,1,1,32]{4,3,2,1,0:T(1,128)} %stack.251) | copy-start | bytes 388
  178.7 15.3 %copy-start.24 = (f32[1,1,1,1,32]{4,3,2,1,0:T(1,128)S(1)}, f32[1,1,1,1,32]{4,3,2,1,0:T(1,128)}, u32[]{:S(2)}) copy-start(f32[1,1,1,1,32]{4,3,2,1,0:T(1,128)} %stack.252) | copy-start | bytes 388
  178.7 15.3 %copy-start.25 = (f32[1,1,1,1,32]{4,3,2,1,0:T(1,128)S(1)}, f32[1,1,1,1,32]{4,3,2,1,0:T(1,128)}, u32[]{:S(2)}) copy-start(f32[1,1,1,1,32]{4,3,2,1,0:T(1,128)} %stack.253) | copy-start | bytes 388
  185.7 18.4 %copy-start.42 = (pred[4,4]{1,0:T(4,128)(4,1)S(1)}, pred[4,4]{1,0:T(4,128)(4,1)}, u32[]{:S(2)}) copy-start(pred[4,4]{1,0:T(4,128)(4,1)} %iota_compare_fusion.1) | copy-start | bytes 52
  185.7 33.9 %copy-start.11 = (f32[16,4,8]{0,2,1:T(8,128)S(1)}, f32[16,4,8]{0,2,1:T(8,128)}, u32[]{:S(2)}) copy-start(f32[16,4,8]{0,2,1:T(8,128)} %copy-done.10) | copy-start | bytes 6148
  185.7 53.5 %copy-start.13 = (f32[16,4,8]{0,2,1:T(8,128)S(1)}, f32[16,4,8]{0,2,1:T(8,128)}, u32[]{:S(2)}) copy-start(f32[16,4,8]{0,2,1:T(8,128)} %copy-done.12) | copy-start | bytes 6148
  194.1 10.0 %copy-start.14 = (f32[16,1,1,1,32]{4,3,2,1,0:T(1,128)}, f32[16,1,1,1,32]{4,3,2,1,0:T(1,128)S(1)}, u32[]{:S(2)}) copy-start(f32[16,1,1,1,32]{4,3,2,1,0:T(1,128)S(1)} %constant_dynamic-update-slice_fusion.32) | copy-start | bytes 6148
  205.6 9.9 %all-to-all-start = ((f32[16,1,1,32]{3,2,1,0:T(1,128)}), f32[16,1,1,32]{3,2,1,0:T(1,128)S(1)}, u32[]{:S(2)}, u32[]{:S(2)}) async-start(f32[16,1,1,32]{3,2,1,0:T(1,128)} %copy.169), calls=%async_computation | async-start | bytes 16384 | tf_op jit(solution)/shard_map/all_to_all | solution.py:125
  215.5 9.8 %all-to-all-start.4 = ((f32[16,1,1,1,32]{4,3,2,1,0:T(1,128)}), f32[16,1,1,1,32]{4,3,2,1,0:T(1,128)S(1)}, u32[]{:S(2)}, u32[]{:S(2)}) async-start(f32[16,1,1,1,32]{4,3,2,1,0:T(1,128)} %constant_dynamic-update-slice_fusion.16), calls=%async_computation.4 | async-start | bytes 16384 | tf_op jit(solution)/shard_map/all_to_all | solution.py:19
  225.3 9.9 %all-to-all-start.3 = ((f32[16,1,1,32]{3,2,1,0:T(1,128)}), f32[16,1,1,32]{3,2,1,0:T(1,128)S(1)}, u32[]{:S(2)}, u32[]{:S(2)}) async-start(f32[16,1,1,32]{3,2,1,0:T(1,128)} %copy.174), calls=%async_computation.3 | async-start | bytes 16384 | tf_op jit(solution)/shard_map/all_to_all | solution.py:125
  235.2 9.8 %all-to-all-start.7 = ((f32[16,1,1,1,32]{4,3,2,1,0:T(1,128)}), f32[16,1,1,1,32]{4,3,2,1,0:T(1,128)S(1)}, u32[]{:S(2)}, u32[]{:S(2)}) async-start(f32[16,1,1,1,32]{4,3,2,1,0:T(1,128)} %copy-done.14), calls=%async_computation.7 | async-start | bytes 16384 | tf_op jit(solution)/shard_map/all_to_all | solution.py:19
  245.0 11.0 %all-to-all-start.6 = ((f32[16,1,1,32]{3,2,1,0:T(1,128)}), f32[16,1,1,32]{3,2,1,0:T(1,128)S(1)}, u32[]{:S(2)}, u32[]{:S(2)}) async-start(f32[16,1,1,32]{3,2,1,0:T(1,128)} %copy.179), calls=%async_computation.6 | async-start | bytes 16384 | tf_op jit(solution)/shard_map/all_to_all | solution.py:125
  256.0 29.3 %copy-start.8 = (f32[16,1,1,32]{3,2,1,0:T(1,128)}, f32[16,1,1,32]{3,2,1,0:T(1,128)S(1)}, u32[]{:S(2)}) copy-start(f32[16,1,1,32]{3,2,1,0:T(1,128)S(1)} %all-to-all-done.6) | copy-start | bytes 6148
  256.0 12.4 %all-to-all-start.10 = ((f32[16,1,1,1,32]{4,3,2,1,0:T(1,128)}), f32[16,1,1,1,32]{4,3,2,1,0:T(1,128)S(1)}, u32[]{:S(2)}, u32[]{:S(2)}) async-start(f32[16,1,1,1,32]{4,3,2,1,0:T(1,128)} %constant_dynamic-update-slice_fusion.48), calls=%async_computation.10 | async-start | bytes 16384 | tf_op jit(solution)/shard_map/all_to_all | solution.py:19
  265.7 19.2 %copy-start.16 = (bf16[1,4,512]{2,1,0:T(4,128)(2,1)S(1)}, bf16[1,4,512]{2,1,0:T(4,128)(2,1)}, u32[]{:S(2)}) copy-start(bf16[1,4,512]{2,1,0:T(4,128)(2,1)} %param.22) | copy-start | bytes 12292
  268.4 10.3 %all-to-all-start.9 = ((f32[16,1,1,32]{3,2,1,0:T(1,128)}), f32[16,1,1,32]{3,2,1,0:T(1,128)S(1)}, u32[]{:S(2)}, u32[]{:S(2)}) async-start(f32[16,1,1,32]{3,2,1,0:T(1,128)} %copy.184), calls=%async_computation.9 | async-start | bytes 16384 | tf_op jit(solution)/shard_map/all_to_all | solution.py:125
  278.7 13.5 %copy-start.9 = (f32[16,1,1,32]{3,2,1,0:T(1,128)}, f32[16,1,1,32]{3,2,1,0:T(1,128)S(1)}, u32[]{:S(2)}) copy-start(f32[16,1,1,32]{3,2,1,0:T(1,128)S(1)} %all-to-all-done.9) | copy-start | bytes 6148
  278.7 13.5 %all-to-all-start.2 = ((f32[16,1,1,4096]{3,1,2,0:T(1,128)}), f32[16,1,1,4096]{3,1,2,0:T(1,128)S(1)}, u32[]{:S(2)}, u32[]{:S(2)}) async-start(f32[16,1,1,4096]{3,1,2,0:T(1,128)} %bitcast.18), calls=%async_computation.2 | async-start | bytes 524288 | tf_op jit(solution)/shard_map/all_to_all | solution.py:123
  282.2 52.2 %copy-start.1 = (bf16[1920,512]{1,0:T(8,128)(2,1)S(1)}, bf16[1920,512]{1,0:T(8,128)(2,1)}, u32[]{:S(2)}) copy-start(bf16[1920,512]{1,0:T(8,128)(2,1)} %param.16) | copy-start | bytes 5898244
  292.2 13.5 %all-to-all-start.5 = ((f32[16,1,1,4096]{3,1,2,0:T(1,128)}), f32[16,1,1,4096]{3,1,2,0:T(1,128)S(1)}, u32[]{:S(2)}, u32[]{:S(2)}) async-start(f32[16,1,1,4096]{3,1,2,0:T(1,128)} %bitcast.33), calls=%async_computation.5 | async-start | bytes 524288 | tf_op jit(solution)/shard_map/all_to_all | solution.py:123
  305.8 13.5 %all-to-all-start.8 = ((f32[16,1,1,4096]{3,1,2,0:T(1,128)}), f32[16,1,1,4096]{3,1,2,0:T(1,128)S(1)}, u32[]{:S(2)}, u32[]{:S(2)}) async-start(f32[16,1,1,4096]{3,1,2,0:T(1,128)} %bitcast.47), calls=%async_computation.8 | async-start | bytes 524288 | tf_op jit(solution)/shard_map/all_to_all | solution.py:123
  319.3 13.5 %all-to-all-start.11 = ((f32[16,1,1,4096]{3,1,2,0:T(1,128)}), f32[16,1,1,4096]{3,1,2,0:T(1,128)S(1)}, u32[]{:S(2)}, u32[]{:S(2)}) async-start(f32[16,1,1,4096]{3,1,2,0:T(1,128)} %bitcast.61), calls=%async_computation.11 | async-start | bytes 524288 | tf_op jit(solution)/shard_map/all_to_all | solution.py:123
